TPU v7x, 32 devices: a whole 2x2x4 slice. The times are simulated.
32 devices in a mesh: dp: 4 (over x, core), uly: 8 (over z, y).
Axes of the slice: x: 2, y: 2, z: 4, core: 2. Of those that a mesh axis runs over, the one named last changes fastest.
Arguments:
- queries: bfloat16 [4, 1024, 4096], P('dp', 'uly'), may hold values from -6 to 6
- key_rows: bfloat16 [4, 1024, 4096], P('dp', 'uly'), may hold values from -5 to 5
- value_rows: bfloat16 [4, 1024, 4096], P('dp', 'uly'), may hold values from -5 to 5
- out_grad: bfloat16 [4, 1024, 4096], P('dp', 'uly'), may hold values from -5 to 5
- prev_grads: bfloat16 [4, 5120, 2048], P('dp', None, 'uly'), may hold values from -1.5 to 1.5
Outputs:
- attended: bfloat16 [4, 1024, 4096], P('dp', 'uly')
- query_grad: bfloat16 [4, 1024, 4096], P('dp', 'uly')
- key_grad: bfloat16 [4, 1024, 4096], P('dp', 'uly')
- value_grad: bfloat16 [4, 1024, 4096], P('dp', 'uly')
- grad_sum: float32 [5120, 2048], P('dp', 'uly')
All inputs are finite; a program needn't handle non-finite values.
Results may differ from a plain program's by a relative error of at most 0.012.
Values may be sent and summed in bfloat16 or wider, within the bound.
A program may use at most 128 MiB of HBM per device.

v0:
```python
import functools
import math

import jax
import jax.numpy as jnp
from jax import lax
from jax.experimental import pallas as pl
from jax.experimental.pallas import tpu as pltpu
from jax.sharding import PartitionSpec as P

HD = 128
VMEM_BYTES = 67043328
MESH = pl.DeviceIdType.MESH
TRANS_B = (((1,), (1,)), ((), ()))
TRANS_A = (((0,), (0,)), ((), ()))


def dot(left, right):
    return jnp.dot(left, right, preferred_element_type=jnp.float32)


def dot_tb(left, right):
    return lax.dot_general(left, right, TRANS_B, preferred_element_type=jnp.float32)


def dot_ta(left, right):
    return lax.dot_general(left, right, TRANS_A, preferred_element_type=jnp.float32)


def far_first(count):
    return sorted(range(1, count), key=lambda step: (-min(step, count - step), step))


def kernel(
    dp_count,
    uly_count,
    block_rows,
    sum_rows,
    q_ref,
    k_ref,
    v_ref,
    g_ref,
    prev_ref,
    out_o,
    out_dq,
    out_dk,
    out_dv,
    out_sum,
    held,
    made,
    dk_acc,
    dv_acc,
    grad_in,
    in_send,
    in_recv,
    out_send,
    out_recv,
    grad_send,
    grad_recv,
):
    me_dp = lax.axis_index("dp")
    me = lax.axis_index("uly")
    heads = held.shape[0]
    tok_rows = held.shape[3]
    seq = uly_count * tok_rows
    rows = grad_in.shape[1]
    sources = (q_ref, k_ref, v_ref, g_ref)
    targets = (out_o, out_dq, out_dk, out_dv)
    uly_steps = far_first(uly_count)
    dp_steps = far_first(dp_count)

    barrier = pltpu.get_barrier_semaphore()
    for step in uly_steps:
        peer = lax.rem(me + step, uly_count)
        pl.semaphore_signal(barrier, inc=1, device_id=(me_dp, peer), device_id_type=MESH)
    for step in dp_steps:
        peer = lax.rem(me_dp + step, dp_count)
        pl.semaphore_signal(barrier, inc=1, device_id=(peer, me), device_id_type=MESH)
    pl.semaphore_wait(barrier, uly_count + dp_count - 2)

    def columns(owner, head):
        return pl.ds(pl.multiple_of((owner * heads + head) * HD, HD), HD)

    def send_inputs(head, carry):
        for step in uly_steps:
            peer = lax.rem(me + step, uly_count)
            for which in range(4):
                pltpu.make_async_remote_copy(
                    src_ref=sources[which].at[0, :, columns(peer, head)],
                    dst_ref=held.at[head, which, me],
                    send_sem=in_send,
                    recv_sem=in_recv.at[head],
                    device_id=(me_dp, peer),
                    device_id_type=MESH,
                ).start()
        for which in range(4):
            pltpu.make_async_copy(
                sources[which].at[0, :, columns(me, head)],
                held.at[head, which, me],
                in_recv.at[head],
            ).start()
        return carry

    lax.fori_loop(0, heads, send_inputs, 0)

    for step in dp_steps:
        peer = lax.rem(me_dp + step, dp_count)
        pltpu.make_async_remote_copy(
            src_ref=prev_ref.at[0, pl.ds(pl.multiple_of(peer * rows, 16), rows), :],
            dst_ref=grad_in.at[me_dp],
            send_sem=grad_send,
            recv_sem=grad_recv,
            device_id=(peer, me),
            device_id_type=MESH,
        ).start()
    pltpu.make_async_copy(
        prev_ref.at[0, pl.ds(pl.multiple_of(me_dp * rows, 16), rows), :],
        grad_in.at[me_dp],
        grad_recv,
    ).start()

    def send_outputs(head):
        for step in uly_steps:
            peer = lax.rem(me + step, uly_count)
            for which in range(4):
                pltpu.make_async_remote_copy(
                    src_ref=made.at[head, which, peer],
                    dst_ref=targets[which].at[0, :, columns(me, head)],
                    send_sem=out_send,
                    recv_sem=out_recv.at[which],
                    device_id=(me_dp, peer),
                    device_id_type=MESH,
                ).start()
        for which in range(4):
            pltpu.make_async_copy(
                made.at[head, which, me],
                targets[which].at[0, :, columns(me, head)],
                out_recv.at[which],
            ).start()

    score_scale = 1.0 / math.sqrt(HD)
    per_block = block_rows // tok_rows

    def one_head(head, carry):
        pltpu.make_async_copy(held.at[head], held.at[head], in_recv.at[head]).wait()
        keys = held[head, 1].reshape(seq, HD)
        values = held[head, 2].reshape(seq, HD)
        dk_acc[...] = jnp.zeros_like(dk_acc)
        dv_acc[...] = jnp.zeros_like(dv_acc)

        def one_block(block, inner):
            first = block * per_block
            query = held[head, 0, pl.ds(first, per_block)].reshape(block_rows, HD)
            grad = held[head, 3, pl.ds(first, per_block)].reshape(block_rows, HD)
            scores = dot_tb(query, keys) * score_scale
            row_max = jnp.max(scores, axis=-1, keepdims=True)
            shifted = jnp.exp(scores - row_max)
            prob_rows = shifted * (1.0 / jnp.sum(shifted, axis=-1, keepdims=True))
            prob_low = prob_rows.astype(jnp.bfloat16)
            dprobs = dot_tb(grad, values)
            row_delta = jnp.sum(prob_rows * dprobs, axis=-1, keepdims=True)
            dscores = (prob_rows * (dprobs - row_delta) * score_scale).astype(jnp.bfloat16)
            part = (per_block, tok_rows, HD)
            made[head, 0, pl.ds(first, per_block)] = (
                dot(prob_low, values).astype(jnp.bfloat16).reshape(part)
            )
            made[head, 1, pl.ds(first, per_block)] = (
                dot(dscores, keys).astype(jnp.bfloat16).reshape(part)
            )
            dk_acc[...] += dot_ta(dscores, query)
            dv_acc[...] += dot_ta(prob_low, grad)
            return inner

        lax.fori_loop(0, uly_count // per_block, one_block, 0)
        whole = (uly_count, tok_rows, HD)
        made[head, 2] = dk_acc[...].astype(jnp.bfloat16).reshape(whole)
        made[head, 3] = dv_acc[...].astype(jnp.bfloat16).reshape(whole)

        @pl.when(head > 0)
        def _():
            send_outputs(head - 1)

        return carry

    lax.fori_loop(0, heads, one_head, 0)

    pltpu.make_async_copy(grad_in, grad_in, grad_recv).wait()

    def sum_block(block, carry):
        span = pl.ds(pl.multiple_of(block * sum_rows, 16), sum_rows)
        total = grad_in[0, span].astype(jnp.float32)
        for term in range(1, dp_count):
            total = total + grad_in[term, span].astype(jnp.float32)
        out_sum[span] = total
        return carry

    lax.fori_loop(0, rows // sum_rows, sum_block, 0)
    send_outputs(heads - 1)

    others = pl.ds(0, uly_count - 1)
    sent = held.at[:, :, others]
    pltpu.make_async_copy(sent, sent, in_send).wait()
    grad_sent = grad_in.at[pl.ds(0, dp_count - 1)]
    pltpu.make_async_copy(grad_sent, grad_sent, grad_send).wait()
    for which in range(4):
        pltpu.make_async_copy(targets[which], targets[which], out_recv.at[which]).wait()
    made_sent = made.at[:, :, others]
    pltpu.make_async_copy(made_sent, made_sent, out_send).wait()


def store_all(*refs):
    sems = refs[10]
    copies = [pltpu.make_async_copy(refs[i], refs[5 + i], sems.at[i]) for i in range(5)]
    for copy in copies:
        copy.start()
    for copy in copies:
        copy.wait()


def on_device(queries, key_rows, value_rows, out_grad, prev_grads):
    dp_count = lax.axis_size("dp")
    uly_count = lax.axis_size("uly")
    tok_rows, width = queries.shape[1:]
    heads = width // uly_count // HD
    seq = uly_count * tok_rows
    rows = prev_grads.shape[1] // dp_count
    cols = prev_grads.shape[2]
    per_block = max(1, min(uly_count, 256 // tok_rows))
    while uly_count % per_block:
        per_block -= 1
    sum_rows = math.gcd(rows, 64)
    token_shape = (1, tok_rows, width)
    grant = VMEM_BYTES - 8 * tok_rows * width - 4 * rows * cols - (1 << 19)
    token_out = pltpu.VMEM(token_shape, jnp.bfloat16)
    in_hbm = pl.BlockSpec(memory_space=pltpu.HBM)
    in_vmem = pl.BlockSpec(memory_space=pltpu.VMEM)
    results = pl.pallas_call(
        functools.partial(kernel, dp_count, uly_count, per_block * tok_rows, sum_rows),
        out_shape=(
            token_out,
            token_out,
            token_out,
            token_out,
            pltpu.VMEM((rows, cols), jnp.float32),
        ),
        in_specs=[in_hbm] * 5,
        out_specs=[in_vmem] * 5,
        scratch_shapes=[
            pltpu.VMEM((heads, 4, uly_count, tok_rows, HD), jnp.bfloat16),
            pltpu.VMEM((heads, 4, uly_count, tok_rows, HD), jnp.bfloat16),
            pltpu.VMEM((seq, HD), jnp.float32),
            pltpu.VMEM((seq, HD), jnp.float32),
            pltpu.VMEM((dp_count, rows, cols), jnp.bfloat16),
            pltpu.SemaphoreType.DMA,
            pltpu.SemaphoreType.DMA((heads,)),
            pltpu.SemaphoreType.DMA,
            pltpu.SemaphoreType.DMA((4,)),
            pltpu.SemaphoreType.DMA,
            pltpu.SemaphoreType.DMA,
        ],
        compiler_params=pltpu.CompilerParams(
            collective_id=0, has_side_effects=True, vmem_limit_bytes=grant
        ),
        name="attend",
    )(queries, key_rows, value_rows, out_grad, prev_grads)
    return pl.pallas_call(
        store_all,
        out_shape=tuple(jax.ShapeDtypeStruct(one.shape, one.dtype) for one in results),
        in_specs=[in_vmem] * 5,
        out_specs=[in_hbm] * 5,
        scratch_shapes=[pltpu.SemaphoreType.DMA((5,))],
        compiler_params=pltpu.CompilerParams(vmem_limit_bytes=8 * 1024 * 1024),
        name="store_all",
    )(*results)


def solution(mesh):
    return jax.shard_map(
        on_device,
        mesh=mesh,
        in_specs=(
            P("dp", "uly", None),
            P("dp", "uly", None),
            P("dp", "uly", None),
            P("dp", "uly", None),
            P("dp", None, "uly"),
        ),
        out_specs=(
            P("dp", "uly", None),
            P("dp", "uly", None),
            P("dp", "uly", None),
            P("dp", "uly", None),
            P("dp", "uly"),
        ),
        check_vma=False,
    )
```

profile of v0, /device:TPU:10, one launch (start us, length us, event | category | flops | bytes accessed | tf_op | source)
XLA Modules:
  0.0 187.3 jit_solution(5326559063846966200)
XLA Ops:
  0.6 184.2 %attend.1 = (bf16[1,128,4096]{2,1,0:T(8,128)(2,1)S(1)}, bf16[1,128,4096]{2,1,0:T(8,128)(2,1)S(1)}, bf16[1,128,4096]{2,1,0:T(8,128)(2,1)S(1)}, bf16[1,128,4096]{2,1,0:T(8,128)(2,1)S(1)}, f32[1280,256]{1,0:T(8,128)S(1)}) custom-call(bf16[1,128,4096]{2,1,0:T(8,128)(2,1)} %q_ref.1, bf16[1,128,4096]{2,1,0:T(8,128)(2,1)} %k_ref.1, bf16[1,128,4096]{2,1,0:T(8,128)(2,1)} %v_ref.1, ...), custom_call_target="tpu_custom_call" | custom-call | tf_op jit(solution)/shard_map/attend/pallas_call | solution.py:237
  184.8 2.5 %store_all.1 = (bf16[1,128,4096]{2,1,0:T(8,128)(2,1)}, bf16[1,128,4096]{2,1,0:T(8,128)(2,1)}, bf16[1,128,4096]{2,1,0:T(8,128)(2,1)}, bf16[1,128,4096]{2,1,0:T(8,128)(2,1)}, f32[1280,256]{1,0:T(8,128)}) custom-call(bf16[1,128,4096]{2,1,0:T(8,128)(2,1)S(1)} %get-tuple-element.10.refs_0_, bf16[1,128,4096]{2,1,0:T(8,128)(2,1)S(1)} %get-tuple-element.11.refs_1_, ...), custom_call_target="tpu_custom_call" | custom-call | tf_op jit(solution)/shard_map/store_all/pallas_call | solution.py:266
where the time goes:
time: 189 us; the launch traced here: 187 us
  Pallas kernels  187 us (99%)
    pallas_call x1, Pallas kernels, on_device(): pl.pallas_call(functools.partial(kernel, dp_count, uly_count, per_block *...  184 us

commit v1 on v0

--- a/solution.py
+++ b/solution.py
@@ -57,6 +57,7 @@
     out_recv,
     grad_send,
     grad_recv,
+    ready,
 ):
     me_dp = lax.axis_index("dp")
     me = lax.axis_index("uly")
@@ -66,33 +67,78 @@
     rows = grad_in.shape[1]
     sources = (q_ref, k_ref, v_ref, g_ref)
     targets = (out_o, out_dq, out_dk, out_dv)
-    uly_steps = far_first(uly_count)
     dp_steps = far_first(dp_count)
 
-    barrier = pltpu.get_barrier_semaphore()
-    for step in uly_steps:
-        peer = lax.rem(me + step, uly_count)
-        pl.semaphore_signal(barrier, inc=1, device_id=(me_dp, peer), device_id_type=MESH)
-    for step in dp_steps:
-        peer = lax.rem(me_dp + step, dp_count)
-        pl.semaphore_signal(barrier, inc=1, device_id=(peer, me), device_id_type=MESH)
-    pl.semaphore_wait(barrier, uly_count + dp_count - 2)
+    wide = uly_count // 4
+    plane = me // wide
+    column = lax.rem(me, wide)
+    inner = (plane == 1) | (plane == 2)
+
+    def row(of_plane, first=0):
+        return [of_plane * wide + lax.rem(column + j, wide) for j in range(first, wide)]
+
+    across = row(3 - plane)
+    two_on = row(lax.rem(plane + 2, 4))
+    beside = row(plane + 1 - 2 * lax.rem(plane, 2)) + row(plane, 1)
+    mirror = across[0]
+    far = [jnp.where(inner, b, a) for a, b in zip(across, two_on)]
+    close = [jnp.where(inner, a, b) for a, b in zip(across, two_on)]
 
     def columns(owner, head):
         return pl.ds(pl.multiple_of((owner * heads + head) * HD, HD), HD)
 
+    def send_input(head, peer):
+        for which in range(4):
+            pltpu.make_async_remote_copy(
+                src_ref=sources[which].at[0, :, columns(peer, head)],
+                dst_ref=held.at[head, which, me],
+                send_sem=in_send,
+                recv_sem=in_recv.at[head],
+                device_id=(me_dp, peer),
+                device_id_type=MESH,
+            ).start()
+
+    barrier = pltpu.get_barrier_semaphore()
+
+    def greet(peer):
+        pl.semaphore_signal(barrier, inc=1, device_id=(me_dp, peer), device_id_type=MESH)
+
+    def early(head, carry):
+        send_input(head, mirror)
+        return carry
+
+    @pl.when(inner)
+    def _():
+        greet(mirror)
+        pl.semaphore_wait(barrier, 1)
+        early(0, 0)
+        for peer in row(3) + row(0):
+            greet(peer)
+        lax.fori_loop(1, heads, early, 0)
+        pl.semaphore_wait(ready, 2 * wide)
+
+    @pl.when(jnp.logical_not(inner))
+    def _():
+        for peer in across + row(plane, 1):
+            greet(peer)
+        for step in dp_steps:
+            peer = lax.rem(me_dp + step, dp_count)
+            pl.semaphore_signal(barrier, inc=1, device_id=(peer, me), device_id_type=MESH)
+        pl.semaphore_wait(barrier, uly_count + dp_count - 2)
+        for step in dp_steps:
+            peer = lax.rem(me_dp + step, dp_count)
+            pl.semaphore_signal(ready, inc=1, device_id=(peer, me), device_id_type=MESH)
+        pl.semaphore_wait(ready, dp_count - 1)
+        for peer in row(1) + row(2):
+            pl.semaphore_signal(ready, inc=1, device_id=(me_dp, peer), device_id_type=MESH)
+
     def send_inputs(head, carry):
-        for step in uly_steps:
-            peer = lax.rem(me + step, uly_count)
-            for which in range(4):
-                pltpu.make_async_remote_copy(
-                    src_ref=sources[which].at[0, :, columns(peer, head)],
-                    dst_ref=held.at[head, which, me],
-                    send_sem=in_send,
-                    recv_sem=in_recv.at[head],
-                    device_id=(me_dp, peer),
-                    device_id_type=MESH,
-                ).start()
+        @pl.when(jnp.logical_not(inner))
+        def _():
+            send_input(head, mirror)
+
+        for peer in two_on + across[1:] + beside:
+            send_input(head, peer)
         for which in range(4):
             pltpu.make_async_copy(
                 sources[which].at[0, :, columns(me, head)],
@@ -119,18 +165,22 @@
         grad_recv,
     ).start()
 
+    sends = []
+    for turn in range(6):
+        for which, peers in ((turn - 1, beside), (turn, far), (turn - 2, close[::-1])):
+            if 0 <= which < 4:
+                sends += [(which, peer) for peer in peers]
+
     def send_outputs(head):
-        for step in uly_steps:
-            peer = lax.rem(me + step, uly_count)
-            for which in range(4):
-                pltpu.make_async_remote_copy(
-                    src_ref=made.at[head, which, peer],
-                    dst_ref=targets[which].at[0, :, columns(me, head)],
-                    send_sem=out_send,
-                    recv_sem=out_recv.at[which],
-                    device_id=(me_dp, peer),
-                    device_id_type=MESH,
-                ).start()
+        for which, peer in sends:
+            pltpu.make_async_remote_copy(
+                src_ref=made.at[head, which, peer],
+                dst_ref=targets[which].at[0, :, columns(me, head)],
+                send_sem=out_send,
+                recv_sem=out_recv.at[which],
+                device_id=(me_dp, peer),
+                device_id_type=MESH,
+            ).start()
         for which in range(4):
             pltpu.make_async_copy(
                 made.at[head, which, me],
@@ -257,6 +307,7 @@
             pltpu.SemaphoreType.DMA((4,)),
             pltpu.SemaphoreType.DMA,
             pltpu.SemaphoreType.DMA,
+            pltpu.SemaphoreType.REGULAR,
         ],
         compiler_params=pltpu.CompilerParams(
             collective_id=0, has_side_effects=True, vmem_limit_bytes=grant

time: 189 us -> 187 us (0.989)
  no operation moved by 1% of the time
where the time goes in v1:
time: 187 us
  Pallas kernels  186 us (99%)
    pallas_call x1, Pallas kernels, on_device(): pl.pallas_call(functools.partial(kernel, dp_count, uly_count, per_block *...  183 us

profile of v1, /device:TPU:10, one launch (start us, length us, event | category | flops | bytes accessed | tf_op | source)
XLA Modules:
  0.0 186.6 jit_solution(13124043284868224056)
XLA Ops:
  0.6 183.5 %attend.1 = (bf16[1,128,4096]{2,1,0:T(8,128)(2,1)S(1)}, bf16[1,128,4096]{2,1,0:T(8,128)(2,1)S(1)}, bf16[1,128,4096]{2,1,0:T(8,128)(2,1)S(1)}, bf16[1,128,4096]{2,1,0:T(8,128)(2,1)S(1)}, f32[1280,256]{1,0:T(8,128)S(1)}) custom-call(bf16[1,128,4096]{2,1,0:T(8,128)(2,1)} %q_ref.1, bf16[1,128,4096]{2,1,0:T(8,128)(2,1)} %k_ref.1, bf16[1,128,4096]{2,1,0:T(8,128)(2,1)} %v_ref.1, ...), custom_call_target="tpu_custom_call" | custom-call | tf_op jit(solution)/shard_map/attend/pallas_call | solution.py:287
  184.1 2.5 %store_all.1 = (bf16[1,128,4096]{2,1,0:T(8,128)(2,1)}, bf16[1,128,4096]{2,1,0:T(8,128)(2,1)}, bf16[1,128,4096]{2,1,0:T(8,128)(2,1)}, bf16[1,128,4096]{2,1,0:T(8,128)(2,1)}, f32[1280,256]{1,0:T(8,128)}) custom-call(bf16[1,128,4096]{2,1,0:T(8,128)(2,1)S(1)} %get-tuple-element.10.refs_0_, bf16[1,128,4096]{2,1,0:T(8,128)(2,1)S(1)} %get-tuple-element.11.refs_1_, ...), custom_call_target="tpu_custom_call" | custom-call | tf_op jit(solution)/shard_map/store_all/pallas_call | solution.py:317

commit v2 on v1

--- a/solution.py
+++ b/solution.py
@@ -58,6 +58,8 @@
     grad_send,
     grad_recv,
     ready,
+    staged,
+    stage_sem,
 ):
     me_dp = lax.axis_index("dp")
     me = lax.axis_index("uly")
@@ -74,13 +76,22 @@
     column = lax.rem(me, wide)
     inner = (plane == 1) | (plane == 2)
 
+    mirror = (3 - plane) * wide + column
+    barrier = pltpu.get_barrier_semaphore()
+
+    def greet(peer):
+        pl.semaphore_signal(barrier, inc=1, device_id=(me_dp, peer), device_id_type=MESH)
+
+    @pl.when(inner)
+    def _():
+        greet(mirror)
+
     def row(of_plane, first=0):
         return [of_plane * wide + lax.rem(column + j, wide) for j in range(first, wide)]
 
     across = row(3 - plane)
     two_on = row(lax.rem(plane + 2, 4))
     beside = row(plane + 1 - 2 * lax.rem(plane, 2)) + row(plane, 1)
-    mirror = across[0]
     far = [jnp.where(inner, b, a) for a, b in zip(across, two_on)]
     close = [jnp.where(inner, a, b) for a, b in zip(across, two_on)]
 
@@ -98,20 +109,35 @@
                 device_id_type=MESH,
             ).start()
 
-    barrier = pltpu.get_barrier_semaphore()
-
-    def greet(peer):
-        pl.semaphore_signal(barrier, inc=1, device_id=(me_dp, peer), device_id_type=MESH)
-
     def early(head, carry):
         send_input(head, mirror)
         return carry
 
-    @pl.when(inner)
-    def _():
-        greet(mirror)
+    @pl.when(plane == 1)
+    def _():
+        for which in range(4):
+            pltpu.make_async_copy(
+                sources[which].at[0, :, columns(mirror, 0)], staged.at[which], stage_sem
+            ).start()
+        pltpu.make_async_copy(staged, staged, stage_sem).wait()
+        pl.semaphore_wait(barrier, 1)
+        for which in range(4):
+            pltpu.make_async_remote_copy(
+                src_ref=staged.at[which],
+                dst_ref=held.at[0, which, me],
+                send_sem=in_send,
+                recv_sem=in_recv.at[0],
+                device_id=(me_dp, mirror),
+                device_id_type=MESH,
+            ).start()
+
+    @pl.when(plane == 2)
+    def _():
         pl.semaphore_wait(barrier, 1)
         early(0, 0)
+
+    @pl.when(inner)
+    def _():
         for peer in row(3) + row(0):
             greet(peer)
         lax.fori_loop(1, heads, early, 0)
@@ -149,21 +175,22 @@
 
     lax.fori_loop(0, heads, send_inputs, 0)
 
-    for step in dp_steps:
-        peer = lax.rem(me_dp + step, dp_count)
-        pltpu.make_async_remote_copy(
-            src_ref=prev_ref.at[0, pl.ds(pl.multiple_of(peer * rows, 16), rows), :],
-            dst_ref=grad_in.at[me_dp],
-            send_sem=grad_send,
-            recv_sem=grad_recv,
-            device_id=(peer, me),
-            device_id_type=MESH,
+    def send_grads():
+        for step in dp_steps:
+            peer = lax.rem(me_dp + step, dp_count)
+            pltpu.make_async_remote_copy(
+                src_ref=prev_ref.at[0, pl.ds(pl.multiple_of(peer * rows, 16), rows), :],
+                dst_ref=grad_in.at[me_dp],
+                send_sem=grad_send,
+                recv_sem=grad_recv,
+                device_id=(peer, me),
+                device_id_type=MESH,
+            ).start()
+        pltpu.make_async_copy(
+            prev_ref.at[0, pl.ds(pl.multiple_of(me_dp * rows, 16), rows), :],
+            grad_in.at[me_dp],
+            grad_recv,
         ).start()
-    pltpu.make_async_copy(
-        prev_ref.at[0, pl.ds(pl.multiple_of(me_dp * rows, 16), rows), :],
-        grad_in.at[me_dp],
-        grad_recv,
-    ).start()
 
     sends = []
     for turn in range(6):
@@ -177,7 +204,7 @@
                 src_ref=made.at[head, which, peer],
                 dst_ref=targets[which].at[0, :, columns(me, head)],
                 send_sem=out_send,
-                recv_sem=out_recv.at[which],
+                recv_sem=out_recv,
                 device_id=(me_dp, peer),
                 device_id_type=MESH,
             ).start()
@@ -185,7 +212,7 @@
             pltpu.make_async_copy(
                 made.at[head, which, me],
                 targets[which].at[0, :, columns(me, head)],
-                out_recv.at[which],
+                out_recv,
             ).start()
 
     score_scale = 1.0 / math.sqrt(HD)
@@ -230,6 +257,10 @@
         def _():
             send_outputs(head - 1)
 
+        @pl.when(head == min(2, heads - 1))
+        def _():
+            send_grads()
+
         return carry
 
     lax.fori_loop(0, heads, one_head, 0)
@@ -252,8 +283,7 @@
     pltpu.make_async_copy(sent, sent, in_send).wait()
     grad_sent = grad_in.at[pl.ds(0, dp_count - 1)]
     pltpu.make_async_copy(grad_sent, grad_sent, grad_send).wait()
-    for which in range(4):
-        pltpu.make_async_copy(targets[which], targets[which], out_recv.at[which]).wait()
+    pltpu.make_async_copy(made, made, out_recv).wait()
     made_sent = made.at[:, :, others]
     pltpu.make_async_copy(made_sent, made_sent, out_send).wait()
 
@@ -304,10 +334,12 @@
             pltpu.SemaphoreType.DMA,
             pltpu.SemaphoreType.DMA((heads,)),
             pltpu.SemaphoreType.DMA,
-            pltpu.SemaphoreType.DMA((4,)),
+            pltpu.SemaphoreType.DMA,
             pltpu.SemaphoreType.DMA,
             pltpu.SemaphoreType.DMA,
             pltpu.SemaphoreType.REGULAR,
+            pltpu.VMEM((4, tok_rows, HD), jnp.bfloat16),
+            pltpu.SemaphoreType.DMA,
         ],
         compiler_params=pltpu.CompilerParams(
             collective_id=0, has_side_effects=True, vmem_limit_bytes=grant

time: 187 us -> 187 us (level)
  no operation moved by 1% of the time
where the time goes in v2:
time: 187 us
  Pallas kernels  186 us (99%)
    pallas_call x1, Pallas kernels, on_device(): pl.pallas_call(functools.partial(kernel, dp_count, uly_count, per_block *...  183 us

profile of v2, /device:TPU:10, one launch (start us, length us, event | category | flops | bytes accessed | tf_op | source)
XLA Modules:
  0.0 186.6 jit_solution(1543027048553185339)
XLA Ops:
  0.6 183.4 %attend.1 = (bf16[1,128,4096]{2,1,0:T(8,128)(2,1)S(1)}, bf16[1,128,4096]{2,1,0:T(8,128)(2,1)S(1)}, bf16[1,128,4096]{2,1,0:T(8,128)(2,1)S(1)}, bf16[1,128,4096]{2,1,0:T(8,128)(2,1)S(1)}, f32[1280,256]{1,0:T(8,128)S(1)}) custom-call(bf16[1,128,4096]{2,1,0:T(8,128)(2,1)} %q_ref.1, bf16[1,128,4096]{2,1,0:T(8,128)(2,1)} %k_ref.1, bf16[1,128,4096]{2,1,0:T(8,128)(2,1)} %v_ref.1, ...), custom_call_target="tpu_custom_call" | custom-call | tf_op jit(solution)/shard_map/attend/pallas_call | solution.py:317
  184.1 2.5 %store_all.1 = (bf16[1,128,4096]{2,1,0:T(8,128)(2,1)}, bf16[1,128,4096]{2,1,0:T(8,128)(2,1)}, bf16[1,128,4096]{2,1,0:T(8,128)(2,1)}, bf16[1,128,4096]{2,1,0:T(8,128)(2,1)}, f32[1280,256]{1,0:T(8,128)}) custom-call(bf16[1,128,4096]{2,1,0:T(8,128)(2,1)S(1)} %get-tuple-element.10.refs_0_, bf16[1,128,4096]{2,1,0:T(8,128)(2,1)S(1)} %get-tuple-element.11.refs_1_, ...), custom_call_target="tpu_custom_call" | custom-call | tf_op jit(solution)/shard_map/store_all/pallas_call | solution.py:349

commit v3 on v1

--- a/solution.py
+++ b/solution.py
@@ -41,10 +41,7 @@
     v_ref,
     g_ref,
     prev_ref,
-    out_o,
-    out_dq,
-    out_dk,
-    out_dv,
+    out_all,
     out_sum,
     held,
     made,
@@ -66,7 +63,6 @@
     seq = uly_count * tok_rows
     rows = grad_in.shape[1]
     sources = (q_ref, k_ref, v_ref, g_ref)
-    targets = (out_o, out_dq, out_dk, out_dv)
     dp_steps = far_first(dp_count)
 
     wide = uly_count // 4
@@ -165,28 +161,19 @@
         grad_recv,
     ).start()
 
-    sends = []
-    for turn in range(6):
-        for which, peers in ((turn - 1, beside), (turn, far), (turn - 2, close[::-1])):
-            if 0 <= which < 4:
-                sends += [(which, peer) for peer in peers]
-
     def send_outputs(head):
-        for which, peer in sends:
+        for peer in beside[wide:] + far + beside[:wide] + close[::-1]:
             pltpu.make_async_remote_copy(
-                src_ref=made.at[head, which, peer],
-                dst_ref=targets[which].at[0, :, columns(me, head)],
+                src_ref=made.at[head, :, peer],
+                dst_ref=out_all.at[:, :, columns(me, head)],
                 send_sem=out_send,
-                recv_sem=out_recv.at[which],
+                recv_sem=out_recv,
                 device_id=(me_dp, peer),
                 device_id_type=MESH,
             ).start()
-        for which in range(4):
-            pltpu.make_async_copy(
-                made.at[head, which, me],
-                targets[which].at[0, :, columns(me, head)],
-                out_recv.at[which],
-            ).start()
+        pltpu.make_async_copy(
+            made.at[head, :, me], out_all.at[:, :, columns(me, head)], out_recv
+        ).start()
 
     score_scale = 1.0 / math.sqrt(HD)
     per_block = block_rows // tok_rows
@@ -252,15 +239,17 @@
     pltpu.make_async_copy(sent, sent, in_send).wait()
     grad_sent = grad_in.at[pl.ds(0, dp_count - 1)]
     pltpu.make_async_copy(grad_sent, grad_sent, grad_send).wait()
-    for which in range(4):
-        pltpu.make_async_copy(targets[which], targets[which], out_recv.at[which]).wait()
+    pltpu.make_async_copy(out_all, out_all, out_recv).wait()
     made_sent = made.at[:, :, others]
     pltpu.make_async_copy(made_sent, made_sent, out_send).wait()
 
 
 def store_all(*refs):
-    sems = refs[10]
-    copies = [pltpu.make_async_copy(refs[i], refs[5 + i], sems.at[i]) for i in range(5)]
+    sems = refs[7]
+    copies = [
+        pltpu.make_async_copy(refs[0].at[i], refs[2 + i].at[0], sems.at[i]) for i in range(4)
+    ]
+    copies.append(pltpu.make_async_copy(refs[1], refs[6], sems.at[4]))
     for copy in copies:
         copy.start()
     for copy in copies:
@@ -279,22 +268,17 @@
     while uly_count % per_block:
         per_block -= 1
     sum_rows = math.gcd(rows, 64)
-    token_shape = (1, tok_rows, width)
     grant = VMEM_BYTES - 8 * tok_rows * width - 4 * rows * cols - (1 << 19)
-    token_out = pltpu.VMEM(token_shape, jnp.bfloat16)
     in_hbm = pl.BlockSpec(memory_space=pltpu.HBM)
     in_vmem = pl.BlockSpec(memory_space=pltpu.VMEM)
     results = pl.pallas_call(
         functools.partial(kernel, dp_count, uly_count, per_block * tok_rows, sum_rows),
         out_shape=(
-            token_out,
-            token_out,
-            token_out,
-            token_out,
+            pltpu.VMEM((4, tok_rows, width), jnp.bfloat16),
             pltpu.VMEM((rows, cols), jnp.float32),
         ),
         in_specs=[in_hbm] * 5,
-        out_specs=[in_vmem] * 5,
+        out_specs=[in_vmem] * 2,
         scratch_shapes=[
             pltpu.VMEM((heads, 4, uly_count, tok_rows, HD), jnp.bfloat16),
             pltpu.VMEM((heads, 4, uly_count, tok_rows, HD), jnp.bfloat16),
@@ -304,7 +288,7 @@
             pltpu.SemaphoreType.DMA,
             pltpu.SemaphoreType.DMA((heads,)),
             pltpu.SemaphoreType.DMA,
-            pltpu.SemaphoreType.DMA((4,)),
+            pltpu.SemaphoreType.DMA,
             pltpu.SemaphoreType.DMA,
             pltpu.SemaphoreType.DMA,
             pltpu.SemaphoreType.REGULAR,
@@ -316,8 +300,9 @@
     )(queries, key_rows, value_rows, out_grad, prev_grads)
     return pl.pallas_call(
         store_all,
-        out_shape=tuple(jax.ShapeDtypeStruct(one.shape, one.dtype) for one in results),
-        in_specs=[in_vmem] * 5,
+        out_shape=(jax.ShapeDtypeStruct((1, tok_rows, width), jnp.bfloat16),) * 4
+        + (jax.ShapeDtypeStruct((rows, cols), jnp.float32),),
+        in_specs=[in_vmem] * 2,
         out_specs=[in_hbm] * 5,
         scratch_shapes=[pltpu.SemaphoreType.DMA((5,))],
         compiler_params=pltpu.CompilerParams(vmem_limit_bytes=8 * 1024 * 1024),

time: 187 us -> 187 us (level)
  no operation moved by 1% of the time
where the time goes in v3:
time: 187 us; the launch traced here: 186 us
  Pallas kernels  185 us (99%)
    pallas_call x1, Pallas kernels, on_device(): pl.pallas_call(functools.partial(kernel, dp_count, uly_count, per_block *...  183 us

profile of v3, /device:TPU:10, one launch (start us, length us, event | category | flops | bytes accessed | tf_op | source)
XLA Modules:
  0.0 185.9 jit_solution(4642544653849983879)
XLA Ops:
  0.6 182.7 %attend.1 = (bf16[4,128,4096]{2,1,0:T(8,128)(2,1)S(1)}, f32[1280,256]{1,0:T(8,128)S(1)}) custom-call(bf16[1,128,4096]{2,1,0:T(8,128)(2,1)} %q_ref.1, bf16[1,128,4096]{2,1,0:T(8,128)(2,1)} %k_ref.1, bf16[1,128,4096]{2,1,0:T(8,128)(2,1)} %v_ref.1, bf16[1,128,4096]{2,1,0:T(8,128)(2,1)} %g_ref.1, bf16[1,5120,256]{2,1,0:T(8,128)(2,1)} %prev_ref.1), custom_call_target="tpu_custom_call" | custom-call | tf_op jit(solution)/shard_map/attend/pallas_call | solution.py:274
  183.4 2.5 %store_all.1 = (bf16[1,128,4096]{2,1,0:T(8,128)(2,1)}, bf16[1,128,4096]{2,1,0:T(8,128)(2,1)}, bf16[1,128,4096]{2,1,0:T(8,128)(2,1)}, bf16[1,128,4096]{2,1,0:T(8,128)(2,1)}, f32[1280,256]{1,0:T(8,128)}) custom-call(bf16[4,128,4096]{2,1,0:T(8,128)(2,1)S(1)} %get-tuple-element.7.refs_0_, f32[1280,256]{1,0:T(8,128)S(1)} %get-tuple-element.8.refs_1_), custom_call_target="tpu_custom_call" | custom-call | tf_op jit(solution)/shard_map/store_all/pallas_call | solution.py:301

commit v4 on v3

--- a/solution.py
+++ b/solution.py
@@ -70,13 +70,22 @@
     column = lax.rem(me, wide)
     inner = (plane == 1) | (plane == 2)
 
+    mirror = (3 - plane) * wide + column
+    barrier = pltpu.get_barrier_semaphore()
+
+    def greet(peer):
+        pl.semaphore_signal(barrier, inc=1, device_id=(me_dp, peer), device_id_type=MESH)
+
+    @pl.when(inner)
+    def _():
+        greet(mirror)
+
     def row(of_plane, first=0):
         return [of_plane * wide + lax.rem(column + j, wide) for j in range(first, wide)]
 
     across = row(3 - plane)
     two_on = row(lax.rem(plane + 2, 4))
     beside = row(plane + 1 - 2 * lax.rem(plane, 2)) + row(plane, 1)
-    mirror = across[0]
     far = [jnp.where(inner, b, a) for a, b in zip(across, two_on)]
     close = [jnp.where(inner, a, b) for a, b in zip(across, two_on)]
 
@@ -94,18 +103,12 @@
                 device_id_type=MESH,
             ).start()
 
-    barrier = pltpu.get_barrier_semaphore()
-
-    def greet(peer):
-        pl.semaphore_signal(barrier, inc=1, device_id=(me_dp, peer), device_id_type=MESH)
-
     def early(head, carry):
         send_input(head, mirror)
         return carry
 
     @pl.when(inner)
     def _():
-        greet(mirror)
         pl.semaphore_wait(barrier, 1)
         early(0, 0)
         for peer in row(3) + row(0):
@@ -145,21 +148,22 @@
 
     lax.fori_loop(0, heads, send_inputs, 0)
 
-    for step in dp_steps:
-        peer = lax.rem(me_dp + step, dp_count)
-        pltpu.make_async_remote_copy(
-            src_ref=prev_ref.at[0, pl.ds(pl.multiple_of(peer * rows, 16), rows), :],
-            dst_ref=grad_in.at[me_dp],
-            send_sem=grad_send,
-            recv_sem=grad_recv,
-            device_id=(peer, me),
-            device_id_type=MESH,
+    def send_grads():
+        for step in dp_steps:
+            peer = lax.rem(me_dp + step, dp_count)
+            pltpu.make_async_remote_copy(
+                src_ref=prev_ref.at[0, pl.ds(pl.multiple_of(peer * rows, 16), rows), :],
+                dst_ref=grad_in.at[me_dp],
+                send_sem=grad_send,
+                recv_sem=grad_recv,
+                device_id=(peer, me),
+                device_id_type=MESH,
+            ).start()
+        pltpu.make_async_copy(
+            prev_ref.at[0, pl.ds(pl.multiple_of(me_dp * rows, 16), rows), :],
+            grad_in.at[me_dp],
+            grad_recv,
         ).start()
-    pltpu.make_async_copy(
-        prev_ref.at[0, pl.ds(pl.multiple_of(me_dp * rows, 16), rows), :],
-        grad_in.at[me_dp],
-        grad_recv,
-    ).start()
 
     def send_outputs(head):
         for peer in beside[wide:] + far + beside[:wide] + close[::-1]:
@@ -216,6 +220,10 @@
         @pl.when(head > 0)
         def _():
             send_outputs(head - 1)
+
+        @pl.when(head == min(2, heads - 1))
+        def _():
+            send_grads()
 
         return carry
 

time: 187 us -> 187 us (level)
  no operation moved by 1% of the time
where the time goes in v4:
time: 187 us; the launch traced here: 186 us
  Pallas kernels  185 us (99%)
    pallas_call x1, Pallas kernels, on_device(): pl.pallas_call(functools.partial(kernel, dp_count, uly_count, per_block *...  183 us

profile of v4, /device:TPU:10, one launch (start us, length us, event | category | flops | bytes accessed | tf_op | source)
XLA Modules:
  0.0 185.8 jit_solution(16063663718313211232)
XLA Ops:
  0.6 182.7 %attend.1 = (bf16[4,128,4096]{2,1,0:T(8,128)(2,1)S(1)}, f32[1280,256]{1,0:T(8,128)S(1)}) custom-call(bf16[1,128,4096]{2,1,0:T(8,128)(2,1)} %q_ref.1, bf16[1,128,4096]{2,1,0:T(8,128)(2,1)} %k_ref.1, bf16[1,128,4096]{2,1,0:T(8,128)(2,1)} %v_ref.1, bf16[1,128,4096]{2,1,0:T(8,128)(2,1)} %g_ref.1, bf16[1,5120,256]{2,1,0:T(8,128)(2,1)} %prev_ref.1), custom_call_target="tpu_custom_call" | custom-call | tf_op jit(solution)/shard_map/attend/pallas_call | solution.py:282
  183.4 2.5 %store_all.1 = (bf16[1,128,4096]{2,1,0:T(8,128)(2,1)}, bf16[1,128,4096]{2,1,0:T(8,128)(2,1)}, bf16[1,128,4096]{2,1,0:T(8,128)(2,1)}, bf16[1,128,4096]{2,1,0:T(8,128)(2,1)}, f32[1280,256]{1,0:T(8,128)}) custom-call(bf16[4,128,4096]{2,1,0:T(8,128)(2,1)S(1)} %get-tuple-element.7.refs_0_, f32[1280,256]{1,0:T(8,128)S(1)} %get-tuple-element.8.refs_1_), custom_call_target="tpu_custom_call" | custom-call | tf_op jit(solution)/shard_map/store_all/pallas_call | solution.py:309
